TPU v7x, 32 devices: a whole 2x2x4 slice. The times are simulated.
32 devices in a mesh: dp: 32 (over z, y, x, core).
Axes of the slice: x: 2, y: 2, z: 4, core: 2. Of those that a mesh axis runs over, the one named last changes fastest.
Arguments:
- images: bfloat16 [64, 197, 384], P('dp'), may hold values from -6 to 6
- params: bfloat16 [1777664], P('dp'), may hold values from -1.2 to 1.4
- cotangent: bfloat16 [64, 197, 384], P('dp'), may hold values from -6 to 6
- counts: int32 [32], P('dp'), may hold values from 1 to 2, as said below
Outputs:
- block_out: bfloat16 [64, 197, 384], P('dp')
- image_grad: bfloat16 [64, 197, 384], P('dp')
- param_grad: float32 [1777664], P('dp')
Inputs may be any that keep to these rules, and one draw needn't show every extreme that they name: `counts`: every device has 1 to 2 live images; some device has exactly 2 and some exactly 1.
All inputs are finite; a program needn't handle non-finite values.
Results may differ from a plain program's by a relative error of at most 0.0075.
Values may be sent and summed in bfloat16 or wider, within the bound.
No kernel may reach another device: no remote copies, remote signals or barrier semaphores. Data moves between devices by JAX's collectives and lax.ppermute only.
A program may use at most 128 MiB of HBM per device.

v0:
```python
import jax
import jax.numpy as jnp
from jax import lax
from jax.sharding import PartitionSpec as P

D = 384
HEADS = 6
FF = 1536
TOK = 197
MB = 2
CAP = 1
EPSILON = 1e-06
SQRT_HALF = 0.7071067811865476
INV_ROOT_TAU = 0.3989422804014327


def param_layout():
    return [
        ("w_qkv", (D, 3 * D)),
        ("b_query", (D,)),
        ("b_value", (D,)),
        ("w_out", (D, D)),
        ("b_out", (D,)),
        ("w_up", (D, FF)),
        ("b_up", (FF,)),
        ("w_down", (FF, D)),
        ("b_down", (D,)),
        ("g_first", (D,)),
        ("b_first", (D,)),
        ("g_second", (D,)),
        ("b_second", (D,)),
    ]


def unpack_flat(flat_buffer):
    pieces = {}
    position = 0
    for entry_name, entry_shape in param_layout():
        entry_size = 1
        for extent_value in entry_shape:
            entry_size = entry_size * extent_value
        pieces[entry_name] = flat_buffer[position : position + entry_size].reshape(entry_shape)
        position = position + entry_size
    return pieces


def fetch_weights(params):
    return unpack_flat(lax.all_gather(params, "dp", axis=0, tiled=True))


def standardize(values):
    centre = values - jnp.mean(values, -1, keepdims=True)
    inverse = lax.rsqrt(jnp.mean(centre * centre, -1, keepdims=True) + EPSILON)
    return (centre * inverse, inverse)


def left_product(first, second):
    return lax.dot_general(
        first, second, (((0,), (0,)), ((), ())), preferred_element_type=jnp.float32
    )


def right_product(first, second):
    return lax.dot_general(
        first, second, (((1,), (1,)), ((), ())), preferred_element_type=jnp.float32
    )


def norm_back(grad_normed, normed_rows, inverse, gain):
    scaled = grad_normed * gain
    return inverse * (
        scaled
        - jnp.mean(scaled, -1, keepdims=True)
        - normed_rows * jnp.mean(scaled * normed_rows, -1, keepdims=True)
    )


def gelu_slope(values):
    return 0.5 * (1.0 + lax.erf(values * SQRT_HALF)) + values * INV_ROOT_TAU * jnp.exp(
        -0.5 * values * values
    )


def head_split(values, image_count):
    return values.reshape(image_count, TOK, HEADS, D // HEADS)


def as_float(values):
    return values.astype(jnp.float32)


def forward_pass(weights, image_block):
    image_count = image_block.shape[0]
    scale = float(D // HEADS) ** (-0.5)
    tokens_in = image_block.reshape(-1, D).astype(jnp.float32)
    first_hat, first_inv = standardize(tokens_in)
    normed = (first_hat * as_float(weights["g_first"]) + as_float(weights["b_first"])).astype(
        jnp.bfloat16
    )
    joined = jnp.dot(normed, weights["w_qkv"], preferred_element_type=jnp.float32)
    query = (joined[:, :D] + as_float(weights["b_query"])).astype(jnp.bfloat16)
    keys_all = joined[:, D : 2 * D].astype(jnp.bfloat16)
    values_all = (joined[:, 2 * D :] + as_float(weights["b_value"])).astype(jnp.bfloat16)
    raw_scores = (
        jnp.einsum(
            "bqhd,bkhd->bhqk",
            head_split(query, image_count),
            head_split(keys_all, image_count),
            preferred_element_type=jnp.float32,
        )
        * scale
    )
    peak = jnp.max(raw_scores, -1, keepdims=True)
    log_total = peak + jnp.log(jnp.sum(jnp.exp(raw_scores - peak), -1, keepdims=True))
    probs_low = jnp.exp(raw_scores - log_total).astype(jnp.bfloat16)
    mixed = (
        jnp.einsum(
            "bhqk,bkhd->bqhd",
            probs_low,
            head_split(values_all, image_count),
            preferred_element_type=jnp.float32,
        )
        .reshape(-1, D)
        .astype(jnp.bfloat16)
    )
    middle = tokens_in + (
        jnp.dot(mixed, weights["w_out"], preferred_element_type=jnp.float32)
        + as_float(weights["b_out"])
    )
    second_hat, second_inv = standardize(middle)
    second = (second_hat * as_float(weights["g_second"]) + as_float(weights["b_second"])).astype(
        jnp.bfloat16
    )
    hidden_pre = jnp.dot(second, weights["w_up"], preferred_element_type=jnp.float32) + as_float(
        weights["b_up"]
    )
    hidden = jax.nn.gelu(hidden_pre, approximate=False).astype(jnp.bfloat16)
    result = middle + (
        jnp.dot(hidden, weights["w_down"], preferred_element_type=jnp.float32)
        + as_float(weights["b_down"])
    )
    saved = (
        first_hat,
        first_inv,
        normed,
        query,
        keys_all,
        values_all,
        log_total,
        mixed,
        second_hat,
        second_inv,
        second,
        hidden_pre,
        hidden,
    )
    return (result.astype(jnp.bfloat16).reshape(image_block.shape), saved)


def backward_pass(weights, saved, grad_out):
    (
        first_hat,
        first_inv,
        normed,
        query,
        keys_all,
        values_all,
        log_total,
        mixed,
        second_hat,
        second_inv,
        second,
        hidden_pre,
        hidden,
    ) = saved
    image_count = query.shape[0] // TOK
    scale = float(D // HEADS) ** (-0.5)
    grads = {}
    grad_low = grad_out.astype(jnp.bfloat16)
    grads["w_down"] = left_product(hidden, grad_low)
    grads["b_down"] = jnp.sum(as_float(grad_low), 0)
    grad_pre = (right_product(grad_low, weights["w_down"]) * gelu_slope(hidden_pre)).astype(
        jnp.bfloat16
    )
    grads["w_up"] = left_product(second, grad_pre)
    grads["b_up"] = jnp.sum(as_float(grad_pre), 0)
    grad_second = right_product(grad_pre, weights["w_up"])
    grads["g_second"] = jnp.sum(grad_second * second_hat, 0)
    grads["b_second"] = jnp.sum(grad_second, 0)
    grad_middle = grad_out + norm_back(
        grad_second, second_hat, second_inv, as_float(weights["g_second"])
    )
    grad_attn = grad_middle.astype(jnp.bfloat16)
    grads["w_out"] = left_product(mixed, grad_attn)
    grads["b_out"] = jnp.sum(as_float(grad_attn), 0)
    grad_mixed = head_split(
        right_product(grad_attn, weights["w_out"]).astype(jnp.bfloat16), image_count
    )
    query_heads = head_split(query, image_count)
    key_heads = head_split(keys_all, image_count)
    value_heads = head_split(values_all, image_count)
    raw_scores = (
        jnp.einsum("bqhd,bkhd->bhqk", query_heads, key_heads, preferred_element_type=jnp.float32)
        * scale
    )
    probs = jnp.exp(raw_scores - log_total)
    probs_low = probs.astype(jnp.bfloat16)
    grad_values = jnp.einsum(
        "bhqk,bqhd->bkhd", probs_low, grad_mixed, preferred_element_type=jnp.float32
    )
    grad_probs = jnp.einsum(
        "bqhd,bkhd->bhqk", grad_mixed, value_heads, preferred_element_type=jnp.float32
    )
    grad_scores = (probs * (grad_probs - jnp.sum(grad_probs * probs, -1, keepdims=True))).astype(
        jnp.bfloat16
    )
    grad_query = (
        jnp.einsum("bhqk,bkhd->bqhd", grad_scores, key_heads, preferred_element_type=jnp.float32)
        * scale
    )
    grad_keys = (
        jnp.einsum("bhqk,bqhd->bkhd", grad_scores, query_heads, preferred_element_type=jnp.float32)
        * scale
    )
    grad_joined = jnp.concatenate(
        [grad_query.reshape(-1, D), grad_keys.reshape(-1, D), grad_values.reshape(-1, D)], 1
    ).astype(jnp.bfloat16)
    grads["w_qkv"] = left_product(normed, grad_joined)
    joined_sums = jnp.sum(as_float(grad_joined), 0)
    grads["b_query"] = joined_sums[:D]
    grads["b_value"] = joined_sums[2 * D :]
    grad_first = right_product(grad_joined, weights["w_qkv"])
    grads["g_first"] = jnp.sum(grad_first * first_hat, 0)
    grads["b_first"] = jnp.sum(grad_first, 0)
    grad_in = grad_middle + norm_back(
        grad_first, first_hat, first_inv, as_float(weights["g_first"])
    )
    return (grads, grad_in.astype(jnp.bfloat16))


def on_device(images, params, cotangent, counts):
    full_length = params.shape[0] * lax.axis_size("dp")
    live_total = counts[0]
    totals = {}
    outputs = []
    in_grads = []
    weights = None
    for micro_step in range(MB):
        weights = fetch_weights(params)
        block_in = images[micro_step * CAP : (micro_step + 1) * CAP]
        result, saved = forward_pass(weights, block_in)
        outputs.append(result)
        weights = unpack_flat(lax.all_gather(params, "dp", axis=0, tiled=True))
        live = (micro_step * CAP + jnp.arange(CAP, dtype=jnp.int32) < live_total).astype(
            jnp.float32
        )
        grad_out = (
            cotangent[micro_step * CAP : (micro_step + 1) * CAP].astype(jnp.float32)
            * live[:, None, None]
        ).reshape(-1, D)
        grads, grad_in = backward_pass(weights, saved, grad_out)
        in_grads.append(grad_in.reshape(block_in.shape))
        for entry_name, entry_shape in param_layout():
            if micro_step == 0:
                totals[entry_name] = grads[entry_name]
            else:
                totals[entry_name] = totals[entry_name] + grads[entry_name]
    pieces = [totals[entry_name].reshape(-1) for entry_name, entry_shape in param_layout()]
    used_length = sum([piece_part.shape[0] for piece_part in pieces])
    pieces.append(jnp.zeros((full_length - used_length,), jnp.float32))
    flat_grad = jnp.concatenate(pieces)
    owned = lax.psum_scatter(flat_grad, "dp", scatter_dimension=0, tiled=True)
    return (jnp.concatenate(outputs, 0), jnp.concatenate(in_grads, 0), owned)


def solution(mesh):
    placed = (P("dp", None, None), P("dp"), P("dp", None, None), P("dp"))
    return jax.shard_map(
        on_device,
        mesh=mesh,
        in_specs=placed,
        out_specs=(P("dp", None, None), P("dp", None, None), P("dp")),
        check_vma=False,
    )
```

profile of v0, /device:TPU:0, one launch (start us, length us, event | category | flops | bytes accessed | tf_op | source)
XLA Modules:
  0.0 429.3 jit_solution(1542696043808574378)
XLA Ops:
  7.2 1.7 reshape.453
  9.7 1.6 fusion.136
  13.5 1.4 convert_reduce_fusion.6
  16.0 70.9 %all-gather.3.cloned.1.call-done = bf16[32,1,55552]{2,1,0:T(2,128)(2,1)} async-done(((bf16[1,1,55552]{2,1,0:T(2,128)(2,1)}), bf16[32,1,55552]{2,1,0:T(2,128)(2,1)}) %all-gather.3.cloned.1.call-update) | async-done | bytes 3555344 | tf_op jit(solution)/shard_map/all_gather | solution.py:48
  86.9 21.3 %reduce.14 = bf16[32,55552]{1,0:T(8,128)(2,1)S(1)} reduce(bf16[32,1,55552]{2,1,0:T(2,128)(2,1)} %all-gather.3.cloned.1.call-done, bf16[]{:T(256)} %constant.101), dimensions={1}, to_apply=%all-gather.reduce_sub_computation | reduce | bytes 7110658 | tf_op jit(solution)/shard_map/all_gather | solution.py:48
  108.2 7.0 %reshape.454 = bf16[1777664]{0:T(1024)(128)(2,1)} reshape(bf16[32,55552]{1,0:T(8,128)(2,1)S(1)} %reduce.14) | data formatting | bytes 7110656
  115.3 1.4 slice_convert_fusion.3
  116.7 1.7 slice.143
  118.4 1.3 slice_convert_fusion.2
  119.7 3.7 fusion.134
  129.9 2.2 reshape.428
  133.6 1.5 reshape.429
  136.2 1.8 copy.61
  138.0 1.7 copy.62
  139.8 1.4 fusion.139
  142.8 3.8 fusion.7
  146.6 3.8 fusion.4
  150.4 1.4 convert_reduce_fusion.1
  153.1 1.5 convert_reduce_fusion
  154.6 1.9 convert_reduce_fusion.9
  159.0 1.7 copy.75
  160.8 2.0 convolution_convert_fusion
  168.7 1.9 fusion.63
  175.8 1.8 convolution_add_fusion
  177.6 2.5 reshape.447
  180.1 3.0 constant_dynamic-update-slice_fusion.9
  183.1 1.3 constant_dynamic-update-slice_fusion.8
  184.4 1.3 constant_dynamic-update-slice_fusion.7
  186.8 1.9 reshape.448
  188.8 3.1 convolution_add_fusion.2
  191.9 2.4 reshape.449
  194.3 1.8 fusion.125
  196.0 2.0 convolution_add_fusion.1
  198.1 3.3 reshape.450
  201.4 2.2 constant_dynamic-update-slice_fusion.6
  203.6 1.3 constant_dynamic-update-slice_fusion.5
  204.9 20.3 %dynamic-update-slice.5 = f32[1777664]{0:T(1024)} dynamic-update-slice(f32[1777664]{0:T(1024)} %constant_dynamic-update-slice_fusion.5, f32[589824]{0:T(1024)S(1)} %reshape.449, s32[]{} %constant.107) | dynamic-update-slice | bytes 4718596
  225.1 1.3 add_dynamic-update-slice_fusion
  226.5 21.2 %dynamic-update-slice.7 = f32[1777664]{0:T(1024)} dynamic-update-slice(f32[1777664]{0:T(1024)} %add_dynamic-update-slice_fusion, f32[589824]{0:T(1024)} %reshape.450, s32[]{} %constant.109) | dynamic-update-slice | bytes 4718596
  247.8 1.3 constant_dynamic-update-slice_fusion.4
  250.1 1.3 constant_dynamic-update-slice_fusion.3
  251.4 1.3 constant_dynamic-update-slice_fusion.2
  252.8 1.3 constant_dynamic-update-slice_fusion.1
  254.1 1.3 constant_dynamic-update-slice_fusion
  255.4 1.3 broadcast_dynamic-update-slice_fusion
  258.0 1.6 fusion.39
  262.4 158.2 %all-reduce.3.cloned.1.call-done = f32[1777664]{0:T(1024)} async-done(((f32[1777664]{0:T(1024)}), f32[1777664]{0:T(1024)}) %all-reduce.3.cloned.1.call-update) | async-done | bytes 7110672
  420.5 1.8 dynamic-slice
  (256 shorter events, 34.6 us)
Async XLA Ops:
  7.2 79.8 %all-gather.3.cloned.1.call-start = ((), (), s32[]{:S(2)}) async-start(), calls=%async_computation | async-start | bytes 7332864 | tf_op jit(solution)/shard_map/all_gather | solution.py:48
  8.9 411.6 %all-reduce.3.cloned.1.call-start = ((), (), s32[]{:S(2)}) async-start(), calls=%async_computation.1 | async-start | bytes 14221312
  9.6 3.4 copy-start.47
  116.7 15.8 %copy-start.64 = (f32[384]{0:T(512)}, f32[384]{0:T(512)S(1)}, u32[]{:S(2)}) copy-start(f32[384]{0:T(512)S(1)} %get-tuple-element.43) | copy-start | bytes 4612
  119.7 3.7 slice-start
  124.4 1.6 copy-start.2
  127.7 4.4 %copy-start.29 = (bf16[197,384]{0,1:T(8,128)(2,1)}, bf16[197,384]{0,1:T(8,128)(2,1)S(1)}, u32[]{:S(2)}) copy-start(bf16[197,384]{0,1:T(8,128)(2,1)S(1)} %copy.65) | copy-start | bytes 453892
  132.1 1.6 copy-start.16
  132.4 2.7 copy-start.27
  132.8 2.3 copy-start.59
  136.2 5.2 %copy-start.31 = (bf16[197,384]{0,1:T(8,128)(2,1)}, bf16[197,384]{0,1:T(8,128)(2,1)S(1)}, u32[]{:S(2)}) copy-start(bf16[197,384]{0,1:T(8,128)(2,1)S(1)} %copy.60) | copy-start | bytes 453892
  142.5 12.0 %copy-start.69 = (f32[197]{0:T(256)}, f32[197]{0:T(256)S(1)}, u32[]{:S(2)}) copy-start(f32[197]{0:T(256)S(1)} %broadcast_multiply_fusion.10) | copy-start | bytes 2368
  142.7 11.8 %copy-start.73 = (f32[197]{0:T(256)}, f32[197]{0:T(256)S(1)}, u32[]{:S(2)}) copy-start(f32[197]{0:T(256)S(1)} %add_rsqrt_fusion.2) | copy-start | bytes 2368
  146.6 3.8 copy-start
  146.6 3.8 copy-start.44
  154.6 2.0 copy-start.20
  160.8 2.0 copy-start.30
  160.8 2.0 copy-start.33
  164.5 8.3 %copy-start.23 = (bf16[6,64,197]{2,1,0:T(8,128)(2,1)}, bf16[6,64,197]{2,1,0:T(8,128)(2,1)S(1)}, u32[]{:S(2)}) copy-start(bf16[6,64,197]{2,1,0:T(8,128)(2,1)S(1)} %fusion.35) | copy-start | bytes 453892
  164.7 8.0 %copy-start.25 = (bf16[6,64,197]{2,1,0:T(8,128)(2,1)}, bf16[6,64,197]{2,1,0:T(8,128)(2,1)S(1)}, u32[]{:S(2)}) copy-start(bf16[6,64,197]{2,1,0:T(8,128)(2,1)S(1)} %fusion.34) | copy-start | bytes 453892
  172.7 2.0 copy-start.49
  172.8 2.0 copy-start.63
  172.8 2.0 copy-start.70
  172.8 2.0 copy-start.74
  180.1 5.6 %copy-start.11 = (f32[197,384]{1,0:T(8,128)S(1)}, f32[197,384]{1,0:T(8,128)}, u32[]{:S(2)}) copy-start(f32[197,384]{1,0:T(8,128)} %copy-done.10) | copy-start | bytes 907780
  180.1 5.6 %copy-start.21 = (f32[384,384]{1,0:T(8,128)S(1)}, f32[384,384]{1,0:T(8,128)}, u32[]{:S(2)}) copy-start(f32[384,384]{1,0:T(8,128)} %fusion.128) | copy-start | bytes 1769476
  180.1 5.6 %copy-start.28 = (bf16[6,64,197]{2,1,0:T(8,128)(2,1)S(1)}, bf16[6,64,197]{2,1,0:T(8,128)(2,1)}, u32[]{:S(2)}) copy-start(bf16[6,64,197]{2,1,0:T(8,128)(2,1)} %copy-done.27) | copy-start | bytes 453892
  185.7 3.1 copy-start.61
  185.7 3.1 copy-start.72
  191.9 2.4 copy-start.45
  194.2 1.8 copy-start.19
  194.3 1.8 copy-start.43
  198.1 5.5 %copy-start.77 = (f32[384]{0:T(512)S(1)}, f32[384]{0:T(512)}, u32[]{:S(2)}) copy-start(f32[384]{0:T(512)} %get-tuple-element.32) | copy-start | bytes 4612
  198.1 5.5 %copy-start.83 = (f32[384]{0:T(512)S(1)}, f32[384]{0:T(512)}, u32[]{:S(2)}) copy-start(f32[384]{0:T(512)} %get-tuple-element.34) | copy-start | bytes 4612
  204.9 20.3 %copy-start.78 = (f32[1536]{0:T(1024)S(1)}, f32[1536]{0:T(1024)}, u32[]{:S(2)}) copy-start(f32[1536]{0:T(1024)} %get-tuple-element.84) | copy-start | bytes 18436
  204.9 20.3 %copy-start.79 = (f32[1536]{0:T(1024)S(1)}, f32[1536]{0:T(1024)}, u32[]{:S(2)}) copy-start(f32[1536]{0:T(1024)} %get-tuple-element.86) | copy-start | bytes 18436
  226.4 21.3 %copy-start.75 = (f32[384]{0:T(512)S(1)}, f32[384]{0:T(512)}, u32[]{:S(2)}) copy-start(f32[384]{0:T(512)} %get-tuple-element.28) | copy-start | bytes 4612
  226.4 21.3 %copy-start.76 = (f32[384]{0:T(512)S(1)}, f32[384]{0:T(512)}, u32[]{:S(2)}) copy-start(f32[384]{0:T(512)} %get-tuple-element.90) | copy-start | bytes 4612
  226.4 22.6 %copy-start.14 = (f32[197,384]{1,0:T(8,128)S(1)}, f32[197,384]{1,0:T(8,128)}, u32[]{:S(2)}) copy-start(f32[197,384]{1,0:T(8,128)} %get-tuple-element.35) | copy-start | bytes 907780
  226.4 22.6 %copy-start.46 = (f32[197,384]{1,0:T(8,128)S(1)}, f32[197,384]{1,0:T(8,128)}, u32[]{:S(2)}) copy-start(f32[197,384]{1,0:T(8,128)} %fusion.131) | copy-start | bytes 907780
  226.4 22.6 %copy-start.50 = (f32[197,384]{1,0:T(8,128)S(1)}, f32[197,384]{1,0:T(8,128)}, u32[]{:S(2)}) copy-start(f32[197,384]{1,0:T(8,128)} %get-tuple-element.83) | copy-start | bytes 907780
  247.7 2.4 copy-start.89
  247.7 3.7 copy-start.88
  247.7 5.1 %copy-start.82 = (f32[384]{0:T(512)S(1)}, f32[384]{0:T(512)}, u32[]{:S(2)}) copy-start(f32[384]{0:T(512)} %get-tuple-element.64) | copy-start | bytes 4612
  247.7 5.1 %copy-start.87 = (f32[384]{0:T(512)S(1)}, f32[384]{0:T(512)}, u32[]{:S(2)}) copy-start(f32[384]{0:T(512)} %get-tuple-element.14) | copy-start | bytes 4612
  247.7 6.4 %copy-start.81 = (f32[384]{0:T(512)S(1)}, f32[384]{0:T(512)}, u32[]{:S(2)}) copy-start(f32[384]{0:T(512)} %get-tuple-element.61) | copy-start | bytes 4612
  247.7 6.4 %copy-start.86 = (f32[384]{0:T(512)S(1)}, f32[384]{0:T(512)}, u32[]{:S(2)}) copy-start(f32[384]{0:T(512)} %get-tuple-element.25) | copy-start | bytes 4612
  256.8 2.8 copy-start.18
  (45 other events, 49.3 us)
Sparse Core Ops, SparseCore 0:
  11.6 75.2 all-gather.2
  256.9 163.5 all-reduce.2
where the time goes:
time: 436 us; the launch traced here: 429 us
  waiting for transfers between devices  229 us (53%)
  local copies, waits for them, and re-layouts  99.4 us (23%)
  other arithmetic  44.2 us (10%)
  matrix products  40.7 us (9%)
  between operations  15.9 us (4%)
    unnamed x3, waiting for transfers between devices  158 us
    all_gather x1, waiting for transfers between devices, fetch_weights(): return unpack_flat(lax.all_gather(params, 'dp', axis=0, tiled=True))  70.9 us
    unnamed x189, local copies, waits for them, and re-layouts  66.8 us
    all_gather x1, other arithmetic, fetch_weights(): return unpack_flat(lax.all_gather(params, 'dp', axis=0, tiled=True))  21.3 us
    dot_general x8, matrix products, left_product(): lax.dot_general(first, second, (((0,), (0,)), ((), ())), preferred_elemen...  12 us
    unnamed x9, other arithmetic  11.8 us
    dot_general x8, matrix products, right_product(): lax.dot_general(first, second, (((1,), (1,)), ((), ())), preferred_elemen...  10.4 us
    reshape x4, local copies, waits for them, and re-layouts, on_device(): totals[entry_name].reshape(-1)  10.1 us
  transfers between devices with their start and end apart: 2, of which 2 were waited for; matrix products, arithmetic and copies ran while one was open for 2% of the time, Pallas kernels for 0%

commit v1 on v0

--- a/solution.py
+++ b/solution.py
@@ -12,6 +12,18 @@
 EPSILON = 1e-06
 SQRT_HALF = 0.7071067811865476
 INV_ROOT_TAU = 0.3989422804014327
+
+
+def collect(value, axis, dim):
+    ways, here, step = (lax.axis_size(axis), lax.axis_index(axis), value.shape[dim])
+    line, have = (value, 1)
+    while have < ways:
+        line = jnp.concatenate(
+            [line, lax.ppermute(line, axis, [(d, (d - have) % ways) for d in range(ways)])],
+            axis=dim,
+        )
+        have = 2 * have
+    return jnp.roll(line, here * step, axis=dim)
 
 
 def param_layout():
@@ -45,7 +57,7 @@
 
 
 def fetch_weights(params):
-    return unpack_flat(lax.all_gather(params, "dp", axis=0, tiled=True))
+    return unpack_flat(collect(params, "dp", 0))
 
 
 def standardize(values):

time: 436 us -> 537 us (1.23)
  waiting for transfers between devices: 229 us -> 273 us
  local copies, waits for them, and re-layouts: 99.4 us -> 126 us
  other arithmetic: 44.2 us -> 57.1 us
  starting transfers between devices: 0.08 us -> 10.9 us
    ppermute x0 -> x5, waiting for transfers between devices: none -> 115 us  [collect(): lax.ppermute(line, axis, [(d, (d - have) % ways) for d in range(ways)])]
    all_gather x1, waiting for transfers between devices: 70.9 us -> 0.01 us  [on_device(): weights = unpack_flat(lax.all_gather(params, 'dp', axis=0, tiled=True))]
    unnamed x189 -> x252, local copies, waits for them, and re-layouts: 66.8 us -> 80 us
    ppermute x0 -> x5, starting transfers between devices: none -> 10.9 us  [collect(): lax.ppermute(line, axis, [(d, (d - have) % ways) for d in range(ways)])]
    reshape x4 -> x8, local copies, waits for them, and re-layouts: 5.88 us -> 15.5 us  [unpack_flat(): flat_buffer[position:position + entry_size].reshape(entry_shape)]
    concatenate x0 -> x4, other arithmetic: none -> 9.08 us  [the longest x1 7.06 us: collect(): return jnp.roll(line, here * step, axis=dim)]
    unnamed x9 -> x11, other arithmetic: 11.8 us -> 11.7 us
  transfers between devices with their start and end apart: 2 -> 7, of which waited for: 2 -> 5; matrix products, arithmetic and copies ran while one was open for 2% -> 13% of each run, Pallas kernels for 0% -> 0%
where the time goes in v1:
time: 537 us; the launch traced here: 528 us
  waiting for transfers between devices  273 us (51%)
  local copies, waits for them, and re-layouts  126 us (23%)
  other arithmetic  57.1 us (11%)
  matrix products  44.7 us (8%)
  between operations  16.3 us (3%)
  starting transfers between devices  10.9 us (2%)
    unnamed x3, waiting for transfers between devices  157 us
    ppermute x5, waiting for transfers between devices, collect(): lax.ppermute(line, axis, [(d, (d - have) % ways) for d in range(ways)])  115 us
    unnamed x252, local copies, waits for them, and re-layouts  80 us
    all_gather x1, other arithmetic, on_device(): weights = unpack_flat(lax.all_gather(params, 'dp', axis=0, tiled=True))  22.7 us
    reshape x8, local copies, waits for them, and re-layouts, unpack_flat(): flat_buffer[position:position + entry_size].reshape(entry_shape)  15.5 us
    dot_general x8, matrix products, right_product(): lax.dot_general(first, second, (((1,), (1,)), ((), ())), preferred_elemen...  12.6 us
    unnamed x11, other arithmetic  11.7 us
    dot_general x8, matrix products, left_product(): lax.dot_general(first, second, (((0,), (0,)), ((), ())), preferred_elemen...  11.2 us
  transfers between devices with their start and end apart: 7, of which 5 were waited for; matrix products, arithmetic and copies ran while one was open for 13% of the time, Pallas kernels for 0%

profile of v1, /device:TPU:0, one launch (start us, length us, event | category | flops | bytes accessed | tf_op | source)
XLA Modules:
  0.0 528.0 jit_solution(13682688024338485169)
XLA Ops:
  7.2 6.4 %collective-permute-start = (bf16[55552]{0:T(1024)(128)(2,1)}, bf16[55552]{0:T(1024)(128)(2,1)S(1)}, u32[]{:S(2)}, u32[]{:S(2)}) collective-permute-start(bf16[55552]{0:T(1024)(128)(2,1)} %param.7), channel_id=1, source_target_pairs={{0,31},{1,0},{2,1},{3,2},{4,3},{5,4},{6,5},{7,6},{8,7},{9,8},{10,9... | collective-permute-start | bytes 333320 | tf_op jit(solution)/shard_map/ppermute | solution.py:22
  13.6 2.7 collective-permute-done
  17.9 5.4 %collective-permute-done.1 = bf16[111104]{0:T(1024)(128)(2,1)S(1)} collective-permute-done((bf16[111104]{0:T(1024)(128)(2,1)S(1)}, bf16[111104]{0:T(1024)(128)(2,1)S(1)}, u32[]{:S(2)}, u32[]{:S(2)}) %collective-permute-start.1) | collective-permute-done | bytes 222240 | tf_op jit(solution)/shard_map/ppermute | solution.py:22
  26.9 2.9 dynamic-update-slice.14
  31.0 2.9 dynamic-update-slice.15
  33.9 2.0 dynamic-update-slice.22
  35.9 4.4 dynamic-update-slice.16
  40.4 1.9 collective-permute-start.3
  43.2 22.2 %collective-permute-done.3 = bf16[444416]{0:T(1024)(128)(2,1)S(1)} collective-permute-done((bf16[444416]{0:T(1024)(128)(2,1)S(1)}, bf16[444416]{0:T(1024)(128)(2,1)S(1)}, u32[]{:S(2)}, u32[]{:S(2)}) %collective-permute-start.3) | collective-permute-done | bytes 888864 | tf_op jit(solution)/shard_map/ppermute | solution.py:22
  71.2 1.4 convert_reduce_fusion.6
  72.6 85.2 %collective-permute-done.4 = bf16[888832]{0:T(1024)(128)(2,1)} collective-permute-done((bf16[888832]{0:T(1024)(128)(2,1)}, bf16[888832]{0:T(1024)(128)(2,1)}, u32[]{:S(2)}, u32[]{:S(2)}) %collective-permute-start.4) | collective-permute-done | bytes 1777696 | tf_op jit(solution)/shard_map/ppermute | solution.py:22
  157.8 2.8 constant_dynamic-update-slice_fusion.4
  160.7 7.1 %fusion = bf16[1777664]{0:T(1024)(128)(2,1)S(1)} fusion(s32[]{:T(128)S(6)} %select_n.11, bf16[1777664]{0:T(1024)(128)(2,1)} %constant_dynamic-update-slice_fusion.4), kind=kLoop, calls=%fused_computation.2 | loop fusion | flops 7110656 | bytes 7110660 | tf_op jit(solution)/shard_map/jit(_roll_dynamic)/concatenate | solution.py:26
  168.4 1.5 slice.155
  169.9 1.6 fusion.136
  171.5 2.1 reshape.433
  176.8 2.2 reshape.438
  186.0 4.2 fusion.5
  191.0 4.7 fusion.8
  196.5 2.1 convolution_add_fusion.1
  198.5 3.2 reshape.464
  201.8 22.7 %reduce.14 = bf16[32,55552]{1,0:T(8,128)(2,1)} reduce(bf16[32,1,55552]{2,1,0:T(2,128)(2,1)} %all-gather.3.cloned.1.call-done, bf16[]{:T(256)} %constant.121), dimensions={1}, to_apply=%all-gather.reduce_sub_computation | reduce | bytes 7110658 | tf_op jit(solution)/shard_map/all_gather | solution.py:265
  224.4 7.7 %reshape.468 = bf16[1777664]{0:T(1024)(128)(2,1)} reshape(bf16[32,55552]{1,0:T(8,128)(2,1)} %reduce.14) | data formatting | bytes 7110656
  233.4 3.7 fusion.135
  237.9 3.1 reshape.446
  241.0 3.6 reshape.447
  244.6 3.2 convert_reduce_fusion
  247.8 1.4 convert_reduce_fusion.1
  250.0 1.9 multiply_reduce_fusion.3
  254.2 1.8 reshape.448
  256.0 2.8 convert_reduce_fusion.9
  259.8 1.7 copy.75
  261.6 2.0 convolution_convert_fusion
  269.9 1.8 fusion.105
  274.9 2.0 reshape.453
  278.3 2.9 fusion.132
  281.2 1.9 convolution_add_fusion
  283.1 2.6 reshape.461
  285.7 3.0 constant_dynamic-update-slice_fusion.14
  292.4 2.0 reshape.462
  294.4 2.0 convolution_add_fusion.2
  296.5 3.3 reshape.463
  301.3 2.0 constant_dynamic-update-slice_fusion.11
  304.6 21.6 %dynamic-update-slice.5 = f32[1777664]{0:T(1024)} dynamic-update-slice(f32[1777664]{0:T(1024)} %constant_dynamic-update-slice_fusion.10, f32[589824]{0:T(1024)} %reshape.463, s32[]{} %constant.127) | dynamic-update-slice | bytes 4718596
  327.5 20.2 %dynamic-update-slice.7 = f32[1777664]{0:T(1024)} dynamic-update-slice(f32[1777664]{0:T(1024)} %add_dynamic-update-slice_fusion, f32[589824]{0:T(1024)S(1)} %copy-done.2, s32[]{} %constant.129) | dynamic-update-slice | bytes 4718596
  357.4 1.6 fusion.40
  362.1 157.1 %all-reduce.3.cloned.1.call-done = f32[1777664]{0:T(1024)} async-done(((f32[1777664]{0:T(1024)}), f32[1777664]{0:T(1024)}) %all-reduce.3.cloned.1.call-update) | async-done | bytes 7110672
  519.2 1.8 dynamic-slice
  (344 shorter events, 61.6 us)
Async XLA Ops:
  7.2 17.6 %copy-start.19 = (bf16[55552]{0:T(1024)(128)(2,1)S(1)}, bf16[55552]{0:T(1024)(128)(2,1)}, u32[]{:S(2)}) copy-start(bf16[55552]{0:T(1024)(128)(2,1)} %param.7) | copy-start | bytes 333316
  7.2 194.6 %all-gather.3.cloned.1.call-start = ((), (), s32[]{:S(2)}) async-start(), calls=%async_computation | async-start | bytes 7332864 | tf_op jit(solution)/shard_map/all_gather | solution.py:265
  7.2 9.1 %collective-permute-start = (bf16[55552]{0:T(1024)(128)(2,1)}, bf16[55552]{0:T(1024)(128)(2,1)S(1)}, u32[]{:S(2)}, u32[]{:S(2)}) collective-permute-start(bf16[55552]{0:T(1024)(128)(2,1)} %param.7), channel_id=1, source_target_pairs={{0,31},{1,0},{2,1},{3,2},{4,3},{5,4},{6,5},{7,6},{8,7},{9,8},{10,9... | collective-permute-start | bytes 333320 | tf_op jit(solution)/shard_map/ppermute | solution.py:22
  17.2 6.0 %collective-permute-start.1 = (bf16[111104]{0:T(1024)(128)(2,1)S(1)}, bf16[111104]{0:T(1024)(128)(2,1)S(1)}, u32[]{:S(2)}, u32[]{:S(2)}) collective-permute-start(bf16[111104]{0:T(1024)(128)(2,1)S(1)} %pad_maximum_fusion.6), channel_id=1, source_target_pairs={{0,30},{1,31},{2,0},{3,1},{4,2},{5,3},{6,4},{7,5},{8,6},{9,7},{10,... | collective-permute-start | bytes 666632 | tf_op jit(solution)/shard_map/ppermute | solution.py:22
  24.2 16.1 %collective-permute-start.2 = (bf16[222208]{0:T(1024)(128)(2,1)S(1)}, bf16[222208]{0:T(1024)(128)(2,1)S(1)}, u32[]{:S(2)}, u32[]{:S(2)}) collective-permute-start(bf16[222208]{0:T(1024)(128)(2,1)S(1)} %pad_maximum_fusion.3), channel_id=1, source_target_pairs={{0,28},{1,29},{2,30},{3,31},{4,0},{5,1},{6,2},{7,3},{8,4},{9,5},{1... | collective-permute-start | bytes 1333256 | tf_op jit(solution)/shard_map/ppermute | solution.py:22
  25.6 493.6 %all-reduce.3.cloned.1.call-start = ((), (), s32[]{:S(2)}) async-start(), calls=%async_computation.1 | async-start | bytes 14221312
  40.4 25.0 %collective-permute-start.3 = (bf16[444416]{0:T(1024)(128)(2,1)S(1)}, bf16[444416]{0:T(1024)(128)(2,1)S(1)}, u32[]{:S(2)}, u32[]{:S(2)}) collective-permute-start(bf16[444416]{0:T(1024)(128)(2,1)S(1)} %pad_maximum_fusion), channel_id=1, source_target_pairs={{0,24},{1,25},{2,26},{3,27},{4,28},{5,29},{6,30},{7,31},{8,0},{9,1... | collective-permute-start | bytes 2666504 | tf_op jit(solution)/shard_map/ppermute | solution.py:22
  65.4 3.6 copy-start.57
  67.7 90.2 %collective-permute-start.4 = (bf16[888832]{0:T(1024)(128)(2,1)}, bf16[888832]{0:T(1024)(128)(2,1)}, u32[]{:S(2)}, u32[]{:S(2)}) collective-permute-start(bf16[888832]{0:T(1024)(128)(2,1)} %copy-done.116), channel_id=1, source_target_pairs={{0,16},{1,17},{2,18},{3,19},{4,20},{5,21},{6,22},{7,23},{8,24},{9,... | collective-permute-start | bytes 5333000 | tf_op jit(solution)/shard_map/ppermute | solution.py:22
  70.3 112.6 %copy-start.7 = (bf16[1,197,384]{2,1,0:T(8,128)(2,1)}, bf16[1,197,384]{2,1,0:T(8,128)(2,1)S(1)}, u32[]{:S(2)}) copy-start(bf16[1,197,384]{2,1,0:T(8,128)(2,1)S(1)} %get-tuple-element.40) | copy-start | bytes 453892
  70.3 199.5 %copy-start.10 = (bf16[1,197,384]{2,1,0:T(8,128)(2,1)}, bf16[1,197,384]{2,1,0:T(8,128)(2,1)S(1)}, u32[]{:S(2)}) copy-start(bf16[1,197,384]{2,1,0:T(8,128)(2,1)S(1)} %get-tuple-element.104) | copy-start | bytes 453892
  70.3 103.4 %copy-start.75 = (f32[197]{0:T(256)}, f32[197]{0:T(256)S(1)}, u32[]{:S(2)}) copy-start(f32[197]{0:T(256)S(1)} %broadcast_multiply_fusion.9) | copy-start | bytes 2368
  70.5 103.7 %copy-start.72 = (f32[197]{0:T(256)}, f32[197]{0:T(256)S(1)}, u32[]{:S(2)}) copy-start(f32[197]{0:T(256)S(1)} %broadcast_multiply_fusion.11) | copy-start | bytes 2368
  72.6 101.1 %copy-start.90 = (f32[197]{0:T(256)}, f32[197]{0:T(256)S(1)}, u32[]{:S(2)}) copy-start(f32[197]{0:T(256)S(1)} %add_rsqrt_fusion.1) | copy-start | bytes 2368
  72.6 101.6 %copy-start.87 = (f32[197]{0:T(256)}, f32[197]{0:T(256)S(1)}, u32[]{:S(2)}) copy-start(f32[197]{0:T(256)S(1)} %add_rsqrt_fusion.3) | copy-start | bytes 2368
  168.4 5.8 %copy-start.69 = (f32[384]{0:T(512)}, f32[384]{0:T(512)S(1)}, u32[]{:S(2)}) copy-start(f32[384]{0:T(512)S(1)} %get-tuple-element.52) | copy-start | bytes 4612
  168.4 22.4 %copy-start.78 = (f32[384]{0:T(512)}, f32[384]{0:T(512)S(1)}, u32[]{:S(2)}) copy-start(f32[384]{0:T(512)S(1)} %get-tuple-element.46) | copy-start | bytes 4612
  175.0 7.5 %copy-start.36 = (bf16[197,384]{0,1:T(8,128)(2,1)}, bf16[197,384]{0,1:T(8,128)(2,1)S(1)}, u32[]{:S(2)}) copy-start(bf16[197,384]{0,1:T(8,128)(2,1)S(1)} %copy.65) | copy-start | bytes 453892
  179.2 5.0 copy-start.34
  183.4 7.4 %copy-start.93 = (f32[197]{0:T(256)}, f32[197]{0:T(256)S(1)}, u32[]{:S(2)}) copy-start(f32[197]{0:T(256)S(1)} %broadcast_multiply_fusion.8) | copy-start | bytes 2368
  185.0 71.1 %copy-start.3 = (f32[197,384]{1,0:T(8,128)}, f32[197,384]{1,0:T(8,128)S(1)}, u32[]{:S(2)}) copy-start(f32[197,384]{1,0:T(8,128)S(1)} %get-tuple-element.90) | copy-start | bytes 907780
  185.0 64.9 %copy-start.96 = (f32[197]{0:T(256)}, f32[197]{0:T(256)S(1)}, u32[]{:S(2)}) copy-start(f32[197]{0:T(256)S(1)} %broadcast_multiply_fusion.10) | copy-start | bytes 2368
  185.2 5.6 %copy-start.98 = (f32[197]{0:T(256)}, f32[197]{0:T(256)S(1)}, u32[]{:S(2)}) copy-start(f32[197]{0:T(256)S(1)} %add_rsqrt_fusion) | copy-start | bytes 2368
  185.2 4.9 copy-start.101
  185.9 4.2 copy-start.54
  191.0 5.5 %copy-start.53 = (bf16[1,197,384]{2,1,0:T(8,128)(2,1)S(1)}, bf16[1,197,384]{2,1,0:T(8,128)(2,1)}, u32[]{:S(2)}) copy-start(bf16[1,197,384]{2,1,0:T(8,128)(2,1)} %get-tuple-element.30) | copy-start | bytes 453892
  233.4 3.8 copy-start.1
  256.0 5.5 %copy-start.68 = (f32[6,197]{1,0:T(8,128)S(1)}, f32[6,197]{1,0:T(8,128)}, u32[]{:S(2)}) copy-start(f32[6,197]{1,0:T(8,128)} %copy-done.67) | copy-start | bytes 14188
  258.8 4.7 copy-start.12
  258.8 4.7 copy-start.37
  267.8 3.9 copy-start.38
  285.7 5.6 %copy-start.13 = (f32[197,384]{1,0:T(8,128)S(1)}, f32[197,384]{1,0:T(8,128)}, u32[]{:S(2)}) copy-start(f32[197,384]{1,0:T(8,128)} %copy-done.12) | copy-start | bytes 907780
  285.7 5.6 %copy-start.27 = (f32[384,384]{1,0:T(8,128)S(1)}, f32[384,384]{1,0:T(8,128)}, u32[]{:S(2)}) copy-start(f32[384,384]{1,0:T(8,128)} %fusion.129) | copy-start | bytes 1769476
  285.7 5.6 %copy-start.33 = (bf16[6,64,197]{2,1,0:T(8,128)(2,1)S(1)}, bf16[6,64,197]{2,1,0:T(8,128)(2,1)}, u32[]{:S(2)}) copy-start(bf16[6,64,197]{2,1,0:T(8,128)(2,1)} %copy-done.32) | copy-start | bytes 453892
  296.4 3.4 copy-start.61
  296.4 3.4 copy-start.64
  296.4 3.4 copy-start.74
  296.5 3.4 copy-start.77
  296.5 3.4 copy-start.89
  304.6 21.6 %copy-start.109 = (f32[1536]{0:T(1024)S(1)}, f32[1536]{0:T(1024)}, u32[]{:S(2)}) copy-start(f32[1536]{0:T(1024)} %get-tuple-element.101) | copy-start | bytes 18436
  304.6 21.6 %copy-start.110 = (f32[1536]{0:T(1024)S(1)}, f32[1536]{0:T(1024)}, u32[]{:S(2)}) copy-start(f32[1536]{0:T(1024)} %get-tuple-element.99) | copy-start | bytes 18436
  304.6 22.9 %copy-start.2 = (f32[589824]{0:T(1024)S(1)}, f32[589824]{0:T(1024)}, u32[]{:S(2)}) copy-start(f32[589824]{0:T(1024)} %reshape.464) | copy-start | bytes 7077892
  327.5 20.2 %copy-start.104 = (f32[384]{0:T(512)S(1)}, f32[384]{0:T(512)}, u32[]{:S(2)}) copy-start(f32[384]{0:T(512)} %get-tuple-element.29) | copy-start | bytes 4612
  327.5 20.2 %copy-start.105 = (f32[384]{0:T(512)S(1)}, f32[384]{0:T(512)}, u32[]{:S(2)}) copy-start(f32[384]{0:T(512)} %get-tuple-element.105) | copy-start | bytes 4612
  327.5 24.1 %copy-start.114 = (f32[384]{0:T(512)S(1)}, f32[384]{0:T(512)}, u32[]{:S(2)}) copy-start(f32[384]{0:T(512)} %get-tuple-element.15) | copy-start | bytes 4612
  327.5 24.1 %copy-start.115 = (f32[384]{0:T(512)S(1)}, f32[384]{0:T(512)}, u32[]{:S(2)}) copy-start(f32[384]{0:T(512)} %get-tuple-element.80) | copy-start | bytes 4612
  327.5 25.4 %copy-start.112 = (f32[384]{0:T(512)S(1)}, f32[384]{0:T(512)}, u32[]{:S(2)}) copy-start(f32[384]{0:T(512)} %get-tuple-element.26) | copy-start | bytes 4612
  327.5 25.4 %copy-start.113 = (f32[384]{0:T(512)S(1)}, f32[384]{0:T(512)}, u32[]{:S(2)}) copy-start(f32[384]{0:T(512)} %get-tuple-element.77) | copy-start | bytes 4612
  (78 other events, 157.9 us)
Sparse Core Ops, SparseCore 0:
  25.8 161.2 all-gather.2
  355.6 163.5 all-reduce.2
